TPU v7x, 32 devices: a whole 2x2x4 slice. The times are simulated.
32 devices in a mesh: group: 4 (over y, x), leaf: 8 (over z, core).
Axes of the slice: x: 2, y: 2, z: 4, core: 2. Of those that a mesh axis runs over, the one named last changes fastest.
Arguments:
- points: bfloat16 [65536, 64], P(('group', 'leaf')), may hold values from -1.1953125 to 1.1953125
- ordering: int32 [32, 2048], P(('group', 'leaf')), may hold values from 0 to 2047, each once within a row
- iterate: float32 [65536, 128], P(('group', 'leaf')), may hold values from -6 to 6
- target: float32 [65536, 128], P(('group', 'leaf')), may hold values from -18 to 18
- step_size: float32 [128], replicated, may hold values from 0.1 to 0.5
- leaf_basis: bfloat16 [65536, 256], P(('group', 'leaf')), may hold values from -0.125 to 0.125
- transfer: bfloat16 [32, 256, 256], P(('group', 'leaf')), may hold values from -0.375 to 0.375
- leaf_skeleton: bfloat16 [32, 256, 64], P(('group', 'leaf')), may hold values from -0.8984375 to 0.8984375
- cluster_skeleton: bfloat16 [4, 256, 64], P('group'), may hold values from -1.1953125 to 1.1953125
- near_table: int32 [32, 8], P(('group', 'leaf')), may hold values from 0 to 1, as said below
- far_table: int32 [32, 8], P(('group', 'leaf')), may hold values from 0 to 1, as said below
- cluster_far: int32 [4, 4], P('group'), may hold values from 0 to 1, as said below
Outputs:
- updated: float32 [65536, 128], P(('group', 'leaf'))
Inputs may be any that keep to these rules, and one draw needn't show every extreme that they name: `near_table`: entries 0 or 1; each leaf's own place is 1; a 1 stands only at places at most 3 away from the leaf's own place; each row has at most 7 ones, and some row exactly 7. `far_table`: entries 0 or 1, never 1 where near_table is 1. `cluster_far`: entries 0 or 1, zero on the diagonal. `ordering`: each row is a permutation.
All inputs are finite; a program needn't handle non-finite values.
Results may differ from a plain program's by a relative error of at most 0.0044.
Values may be sent and summed in bfloat16 or wider, within the bound.
No kernel may reach another device: no remote copies, remote signals or barrier semaphores. Data moves between devices by JAX's collectives and lax.ppermute only.
A program may use at most 128 MiB of HBM per device.

v0:
```python
import jax
import jax.numpy as jnp
from jax import lax
from jax.sharding import PartitionSpec as P

NEAR_MOST = 7


def passed_along(block, axis, distance):
    devices = range(lax.axis_size(axis))
    route = [(i - distance, i) for i in devices if i - distance in devices]
    return lax.ppermute(block, axis, route)


def kernel_tile(left, right):
    left_f = left.astype(jnp.float32)
    right_f = right.astype(jnp.float32)
    left_sq = jnp.sum(left_f * left_f, axis=1)
    right_sq = jnp.sum(right_f * right_f, axis=1)
    inner = lax.dot_general(
        left, right, (((1,), (1,)), ((), ())), preferred_element_type=jnp.float32
    )
    return jnp.exp(-(left_sq[:, None] + right_sq[None, :] - 2.0 * inner)).astype(jnp.bfloat16)


def body(
    points,
    ordering,
    iterate,
    target,
    step_size,
    leaf_basis,
    transfer,
    leaf_skeleton,
    cluster_skeleton,
    near_table,
    far_table,
    cluster_far,
):
    leaf_rows = points.shape[0]
    point_cols = points.shape[1]
    rhs_cols = iterate.shape[1]
    rank_cols = leaf_basis.shape[1]
    rounded = iterate.astype(jnp.bfloat16)
    coeffs = lax.dot_general(
        leaf_basis, rounded, (((0,), (0,)), ((), ())), preferred_element_type=jnp.float32
    ).astype(jnp.bfloat16)
    near_row = near_table[0]
    far_row = far_table[0]
    own_transfer = transfer[0]
    reach = (NEAR_MOST - 1) // 2
    joined = jnp.concatenate([points, rounded], axis=1)
    below_blocks = []
    above_blocks = []
    passing_below = joined
    passing_above = joined
    for distance in range(1, reach + 1):
        passing_below = passed_along(passing_below, "leaf", 1)
        passing_above = passed_along(passing_above, "leaf", -1)
        below_blocks.append(passing_below)
        above_blocks.append(passing_above)
    padded = jnp.concatenate(below_blocks[::-1] + [joined] + above_blocks, axis=0)
    myself = lax.axis_index("leaf")
    cluster_size = near_row.shape[0]

    def window_visit(position, summed):
        place = myself + position - reach
        inside = (place >= 0) & (place < cluster_size)
        listed = lax.dynamic_index_in_dim(
            near_row, jnp.clip(place, 0, cluster_size - 1), 0, keepdims=False
        )
        block = lax.dynamic_slice_in_dim(padded, position * leaf_rows, leaf_rows, 0)
        other_points = block[:, :point_cols]
        other_values = block[:, point_cols:]

        def include(current):
            return current + jnp.dot(
                kernel_tile(points, other_points), other_values, preferred_element_type=jnp.float32
            )

        return lax.cond(inside & (listed > 0), include, lambda current: current, summed)

    near_sum = lax.fori_loop(
        0, 2 * reach + 1, window_visit, jnp.zeros((leaf_rows, rhs_cols), jnp.float32)
    )

    def far_visit(skeletons, values):

        def visit(position, summed):
            listed = lax.dynamic_index_in_dim(far_row, position, 0, keepdims=False)

            def include(current):
                return current + jnp.dot(
                    kernel_tile(leaf_skeleton[0], skeletons[position]),
                    values[position],
                    preferred_element_type=jnp.float32,
                )

            return lax.cond(listed > 0, include, lambda current: current, summed)

        return visit

    empty_far = jnp.zeros((rank_cols, rhs_cols), jnp.float32)
    skeletons = lax.all_gather(leaf_skeleton, "leaf", axis=0, tiled=True)
    values = lax.all_gather(coeffs[None], "leaf", axis=0, tiled=True)
    far_sum = lax.fori_loop(0, skeletons.shape[0], far_visit(skeletons, values), empty_far)
    upward_terms = lax.dot_general(
        own_transfer, coeffs, (((0,), (0,)), ((), ())), preferred_element_type=jnp.float32
    )
    upper = lax.psum(upward_terms, "leaf").astype(jnp.bfloat16)
    cluster_row = cluster_far[0]
    skeletons = lax.all_gather(cluster_skeleton, "group", axis=0, tiled=True)
    values = lax.all_gather(upper[None], "group", axis=0, tiled=True)

    def visit(position, summed):
        listed = lax.dynamic_index_in_dim(cluster_row, position, 0, keepdims=False)

        def include(current):
            return current + jnp.dot(
                kernel_tile(cluster_skeleton[0], skeletons[position]),
                values[position],
                preferred_element_type=jnp.float32,
            )

        return lax.cond(listed > 0, include, lambda current: current, summed)

    lower = lax.fori_loop(0, skeletons.shape[0], visit, empty_far).astype(jnp.bfloat16)
    local = (far_sum + jnp.dot(own_transfer, lower, preferred_element_type=jnp.float32)).astype(
        jnp.bfloat16
    )
    image = jnp.dot(leaf_basis, local, preferred_element_type=jnp.float32) + near_sum
    sorted_target = target[ordering[0]]
    return iterate + step_size[None, :] * (sorted_target - image)


def solution(mesh):
    return jax.shard_map(
        body,
        mesh=mesh,
        in_specs=(
            P(("group", "leaf"), None),
            P(("group", "leaf"), None),
            P(("group", "leaf"), None),
            P(("group", "leaf"), None),
            P(),
            P(("group", "leaf"), None),
            P(("group", "leaf"), None, None),
            P(("group", "leaf"), None, None),
            P("group", None, None),
            P(("group", "leaf"), None),
            P(("group", "leaf"), None),
            P("group", None),
        ),
        out_specs=P(("group", "leaf"), None),
        check_vma=False,
    )
```

profile of v0, /device:TPU:15, one launch (start us, length us, event | category | flops | bytes accessed | tf_op | source)
XLA Modules:
  0.0 278.6 jit_solution(15546868874311557150)
XLA Ops:
  22.8 25.1 %all-reduce.1 = bf16[256,128]{0,1:T(8,128)(2,1)S(1)} all-reduce(f32[256,128]{0,1:T(8,128)S(1)} %convolution_bitcast_fusion.2), channel_id=1, replica_groups=mesh['group'=4,'leaf'=8] {'leaf'}, use_global_device_ids=true, to_apply=%region_6.7 | all-reduce | flops 32768 | bytes 196608 | tf_op jit(solution)/shard_map/psum | solution.py:110
  47.9 17.8 %all-gather = bf16[2048,128]{1,0:T(8,128)(2,1)} all-gather(bf16[256,128]{1,0:T(8,128)(2,1)S(1)} %convolution_convert_fusion), channel_id=2, replica_groups=mesh['group'=4,'leaf'=8] {'leaf'}, dimensions={0}, use_global_device_ids=true | all-gather | bytes 589824 | tf_op jit(solution)/shard_map/all_gather | solution.py:105
  71.9 20.0 %all_gather.12 = bf16[8,256,64]{1,2,0:T(8,128)(2,1)} all-gather(bf16[1,256,64]{1,2,0:T(8,128)(2,1)S(1)} %copy-done.8), channel_id=1, replica_groups=mesh['group'=4,'leaf'=8] {'leaf'}, dimensions={0}, use_global_device_ids=true | all-gather | bytes 294912 | tf_op jit(solution)/shard_map/all_gather | solution.py:104
  95.7 17.8 %while.50 = (s32[]{:T(128)}, f32[256,128]{1,0:T(8,128)}, s32[8]{0:T(128)}, bf16[1,256,64]{2,1,0:T(8,128)(2,1)S(1)}, bf16[8,256,64]{2,1,0:T(8,128)(2,1)}, /*index...) while((s32[]{:T(128)}, f32[256,128]{1,0:T(8,128)}, s32[8]{0:T(128)}, bf16[1,256,64]{2,1,0:T(8,128)(2,1)S(1)}, ...), condition=%wide.region_5.6_spmd, body=%wide.region_0.5_spmd.sunk | while | flops 25624072 | bytes 496837 | solution.py:106
  115.2 13.8 %all-gather.1 = bf16[1024,128]{0,1:T(8,128)(2,1)} all-gather(bf16[256,128]{0,1:T(8,128)(2,1)S(1)} %all-reduce.1), channel_id=3, replica_groups=mesh['group'=4,'leaf'=8] {'group'}, dimensions={0}, use_global_device_ids=true | all-gather | bytes 327680 | tf_op jit(solution)/shard_map/all_gather | solution.py:113
  140.6 7.6 %gather_fusion = f32[2048,128]{1,0:T(8,128)} fusion(f32[2048,128]{1,0:T(8,128)S(1)} %copy-done.1, s32[2048]{0:T(1024)S(1)} %broadcast_clamp_fusion), kind=kCustom, calls=%fused_computation | custom fusion | bytes 2105344 | tf_op jit(solution)/shard_map/gather | solution.py:132
  150.8 9.8 %while.51 = (s32[]{:T(128)}, f32[256,128]{1,0:T(8,128)S(1)}, s32[4]{0:T(128)S(1)}, bf16[1,256,64]{2,1,0:T(8,128)(2,1)S(1)}, bf16[4,256,64]{2,1,0:T(8,128)(2,1)},...) while((s32[]{:T(128)}, f32[256,128]{1,0:T(8,128)S(1)}, s32[4]{0:T(128)S(1)}, ...), condition=%wide.region_12.13_spmd, body=%wide.region_7.12_spmd.sunk | while | flops 25624072 | bytes 496837 | solution.py:127
  160.7 9.4 %collective-permute-start.5 = (bf16[2048,192]{0,1:T(8,128)(2,1)}, bf16[2048,192]{0,1:T(8,128)(2,1)S(1)}, u32[]{:S(2)}, u32[]{:S(2)}) collective-permute-start(bf16[2048,192]{0,1:T(8,128)(2,1)} %collective-permute-done.4), channel_id=1, source_target_pairs={{1,0},{2,1},{3,2},{4,3},{5,4},{6,5},{7,6},{9,8},{10,9},{11,10},{12... | collective-permute-start | bytes 2359304 | tf_op jit(solution)/shard_map/ppermute | solution.py:12
  182.8 9.2 %copy.43 = bf16[14336,192]{1,0:T(8,128)(2,1)} copy(bf16[14336,192]{0,1:T(8,128)(2,1)} %constant_dynamic-update-slice_fusion) | data formatting | bytes 11010048 | tf_op jit(solution)/shard_map/while | solution.py:83
  193.2 77.1 %while.52 = (s32[]{:T(128)}, f32[2048,128]{1,0:T(8,128)}, s32[]{:T(128)}, s32[8]{0:T(128)S(1)}, bf16[2048,64]{1,0:T(8,128)(2,1)S(1)}, /*index=5*/bf16[14336,192]...) while((s32[]{:T(128)}, f32[2048,128]{1,0:T(8,128)}, ...), condition=%wide.region_18.19_spmd, body=%wide.region_13.18_spmd.sunk | while | flops 1632628736 | bytes 3966781 | solution.py:83
  194.5 9.7 %conditional.8 = (f32[2048,128]{1,0:T(8,128)}) conditional(s32[]{:T(128)} %convert_element_type.116, f32[2048,128]{1,0:T(8,128)} %get-tuple-element.708, (bf16[2048,64]{1,0:T(8,128)(2,1)S(1)}, s32[]{:T(128)}, bf16[14336,192]{1,0:T(8,128)(2,1)}, f32[2048,128]{1,0:T(8,128)}) %tuple.139), branch_computations={%region_14.14_spmd, %region_15.17_spmd} | conditional | flops 1632628736 | bytes 3966534 | solution.py:81
  196.2 8.0 %convolution_add_fusion = f32[2048,128]{1,0:T(8,128)} fusion(f32[2048,128]{1,0:T(8,128)} %get-tuple-element.471, bf16[2048,64]{1,0:T(8,128)(2,1)S(1)} %get-tuple-element.472, f32[2048]{0:T(1024)S(1)} %get-tuple-element.582, f32[2048]{0:T(1024)S(1)} %get-tuple-element.583, bf16[14336,192]{1,0:T(8,128)(2,1)} %get-tuple-element.473, s32[]{:T(128)S(6)} %select_n.45, ...), kind=kOutput, calls=%fused_computation.47 | convolution fusion | flops 1631846400 | bytes 3425792 | tf_op jit(solution)/shard_map/while/body/eval_jaxpr/cond/branch_1_fun/dot_general | solution.py:77
  205.5 9.7 %conditional.8 = (f32[2048,128]{1,0:T(8,128)}) conditional(s32[]{:T(128)} %convert_element_type.116, f32[2048,128]{1,0:T(8,128)} %get-tuple-element.708, (bf16[2048,64]{1,0:T(8,128)(2,1)S(1)}, s32[]{:T(128)}, bf16[14336,192]{1,0:T(8,128)(2,1)}, f32[2048,128]{1,0:T(8,128)}) %tuple.139), branch_computations={%region_14.14_spmd, %region_15.17_spmd} | conditional | flops 1632628736 | bytes 3966534 | solution.py:81
  207.2 8.0 %convolution_add_fusion = f32[2048,128]{1,0:T(8,128)} fusion(f32[2048,128]{1,0:T(8,128)} %get-tuple-element.471, bf16[2048,64]{1,0:T(8,128)(2,1)S(1)} %get-tuple-element.472, f32[2048]{0:T(1024)S(1)} %get-tuple-element.582, f32[2048]{0:T(1024)S(1)} %get-tuple-element.583, bf16[14336,192]{1,0:T(8,128)(2,1)} %get-tuple-element.473, s32[]{:T(128)S(6)} %select_n.45, ...), kind=kOutput, calls=%fused_computation.47 | convolution fusion | flops 1631846400 | bytes 3425792 | tf_op jit(solution)/shard_map/while/body/eval_jaxpr/cond/branch_1_fun/dot_general | solution.py:77
  216.5 9.7 %conditional.8 = (f32[2048,128]{1,0:T(8,128)}) conditional(s32[]{:T(128)} %convert_element_type.116, f32[2048,128]{1,0:T(8,128)} %get-tuple-element.708, (bf16[2048,64]{1,0:T(8,128)(2,1)S(1)}, s32[]{:T(128)}, bf16[14336,192]{1,0:T(8,128)(2,1)}, f32[2048,128]{1,0:T(8,128)}) %tuple.139), branch_computations={%region_14.14_spmd, %region_15.17_spmd} | conditional | flops 1632628736 | bytes 3966534 | solution.py:81
  218.2 8.0 %convolution_add_fusion = f32[2048,128]{1,0:T(8,128)} fusion(f32[2048,128]{1,0:T(8,128)} %get-tuple-element.471, bf16[2048,64]{1,0:T(8,128)(2,1)S(1)} %get-tuple-element.472, f32[2048]{0:T(1024)S(1)} %get-tuple-element.582, f32[2048]{0:T(1024)S(1)} %get-tuple-element.583, bf16[14336,192]{1,0:T(8,128)(2,1)} %get-tuple-element.473, s32[]{:T(128)S(6)} %select_n.45, ...), kind=kOutput, calls=%fused_computation.47 | convolution fusion | flops 1631846400 | bytes 3425792 | tf_op jit(solution)/shard_map/while/body/eval_jaxpr/cond/branch_1_fun/dot_general | solution.py:77
  227.5 9.7 %conditional.8 = (f32[2048,128]{1,0:T(8,128)}) conditional(s32[]{:T(128)} %convert_element_type.116, f32[2048,128]{1,0:T(8,128)} %get-tuple-element.708, (bf16[2048,64]{1,0:T(8,128)(2,1)S(1)}, s32[]{:T(128)}, bf16[14336,192]{1,0:T(8,128)(2,1)}, f32[2048,128]{1,0:T(8,128)}) %tuple.139), branch_computations={%region_14.14_spmd, %region_15.17_spmd} | conditional | flops 1632628736 | bytes 3966534 | solution.py:81
  229.2 8.0 %convolution_add_fusion = f32[2048,128]{1,0:T(8,128)} fusion(f32[2048,128]{1,0:T(8,128)} %get-tuple-element.471, bf16[2048,64]{1,0:T(8,128)(2,1)S(1)} %get-tuple-element.472, f32[2048]{0:T(1024)S(1)} %get-tuple-element.582, f32[2048]{0:T(1024)S(1)} %get-tuple-element.583, bf16[14336,192]{1,0:T(8,128)(2,1)} %get-tuple-element.473, s32[]{:T(128)S(6)} %select_n.45, ...), kind=kOutput, calls=%fused_computation.47 | convolution fusion | flops 1631846400 | bytes 3425792 | tf_op jit(solution)/shard_map/while/body/eval_jaxpr/cond/branch_1_fun/dot_general | solution.py:77
  238.5 9.7 %conditional.8 = (f32[2048,128]{1,0:T(8,128)}) conditional(s32[]{:T(128)} %convert_element_type.116, f32[2048,128]{1,0:T(8,128)} %get-tuple-element.708, (bf16[2048,64]{1,0:T(8,128)(2,1)S(1)}, s32[]{:T(128)}, bf16[14336,192]{1,0:T(8,128)(2,1)}, f32[2048,128]{1,0:T(8,128)}) %tuple.139), branch_computations={%region_14.14_spmd, %region_15.17_spmd} | conditional | flops 1632628736 | bytes 3966534 | solution.py:81
  240.2 8.0 %convolution_add_fusion = f32[2048,128]{1,0:T(8,128)} fusion(f32[2048,128]{1,0:T(8,128)} %get-tuple-element.471, bf16[2048,64]{1,0:T(8,128)(2,1)S(1)} %get-tuple-element.472, f32[2048]{0:T(1024)S(1)} %get-tuple-element.582, f32[2048]{0:T(1024)S(1)} %get-tuple-element.583, bf16[14336,192]{1,0:T(8,128)(2,1)} %get-tuple-element.473, s32[]{:T(128)S(6)} %select_n.45, ...), kind=kOutput, calls=%fused_computation.47 | convolution fusion | flops 1631846400 | bytes 3425792 | tf_op jit(solution)/shard_map/while/body/eval_jaxpr/cond/branch_1_fun/dot_general | solution.py:77
  249.5 9.7 %conditional.8 = (f32[2048,128]{1,0:T(8,128)}) conditional(s32[]{:T(128)} %convert_element_type.116, f32[2048,128]{1,0:T(8,128)} %get-tuple-element.708, (bf16[2048,64]{1,0:T(8,128)(2,1)S(1)}, s32[]{:T(128)}, bf16[14336,192]{1,0:T(8,128)(2,1)}, f32[2048,128]{1,0:T(8,128)}) %tuple.139), branch_computations={%region_14.14_spmd, %region_15.17_spmd} | conditional | flops 1632628736 | bytes 3966534 | solution.py:81
  251.2 8.1 %convolution_add_fusion = f32[2048,128]{1,0:T(8,128)} fusion(f32[2048,128]{1,0:T(8,128)} %get-tuple-element.471, bf16[2048,64]{1,0:T(8,128)(2,1)S(1)} %get-tuple-element.472, f32[2048]{0:T(1024)S(1)} %get-tuple-element.582, f32[2048]{0:T(1024)S(1)} %get-tuple-element.583, bf16[14336,192]{1,0:T(8,128)(2,1)} %get-tuple-element.473, s32[]{:T(128)S(6)} %select_n.45, ...), kind=kOutput, calls=%fused_computation.47 | convolution fusion | flops 1631846400 | bytes 3425792 | tf_op jit(solution)/shard_map/while/body/eval_jaxpr/cond/branch_1_fun/dot_general | solution.py:77
  260.5 9.8 %conditional.8 = (f32[2048,128]{1,0:T(8,128)}) conditional(s32[]{:T(128)} %convert_element_type.116, f32[2048,128]{1,0:T(8,128)} %get-tuple-element.708, (bf16[2048,64]{1,0:T(8,128)(2,1)S(1)}, s32[]{:T(128)}, bf16[14336,192]{1,0:T(8,128)(2,1)}, f32[2048,128]{1,0:T(8,128)}) %tuple.139), branch_computations={%region_14.14_spmd, %region_15.17_spmd} | conditional | flops 1632628736 | bytes 3966534 | solution.py:81
  262.2 8.1 %convolution_add_fusion = f32[2048,128]{1,0:T(8,128)} fusion(f32[2048,128]{1,0:T(8,128)} %get-tuple-element.471, bf16[2048,64]{1,0:T(8,128)(2,1)S(1)} %get-tuple-element.472, f32[2048]{0:T(1024)S(1)} %get-tuple-element.582, f32[2048]{0:T(1024)S(1)} %get-tuple-element.583, bf16[14336,192]{1,0:T(8,128)(2,1)} %get-tuple-element.473, s32[]{:T(128)S(6)} %select_n.45, ...), kind=kOutput, calls=%fused_computation.47 | convolution fusion | flops 1631846400 | bytes 3425792 | tf_op jit(solution)/shard_map/while/body/eval_jaxpr/cond/branch_1_fun/dot_general | solution.py:77
  (110 shorter events, 114.6 us)
Async XLA Ops:
  0.0 22.1 %copy-start = (bf16[2048,256]{1,0:T(8,128)(2,1)S(1)}, bf16[2048,256]{1,0:T(8,128)(2,1)}, u32[]{:S(2)}) copy-start(bf16[2048,256]{1,0:T(8,128)(2,1)} %param.29) | copy-start | bytes 3145732
  0.0 91.9 %copy-start.4 = (bf16[2048,64]{0,1:T(8,128)(2,1)S(1)}, bf16[2048,64]{0,1:T(8,128)(2,1)}, u32[]{:S(2)}) copy-start(bf16[2048,64]{0,1:T(8,128)(2,1)} %param.24) | copy-start | bytes 786436
  0.0 22.6 %copy-start.5 = (bf16[1,256,256]{2,1,0:T(8,128)(2,1)S(1)}, bf16[1,256,256]{2,1,0:T(8,128)(2,1)}, u32[]{:S(2)}) copy-start(bf16[1,256,256]{2,1,0:T(8,128)(2,1)} %param.30) | copy-start | bytes 393220
  0.0 71.9 %copy-start.8 = (bf16[1,256,64]{1,2,0:T(8,128)(2,1)S(1)}, bf16[1,256,64]{1,2,0:T(8,128)(2,1)}, u32[]{:S(2)}) copy-start(bf16[1,256,64]{1,2,0:T(8,128)(2,1)} %param.31) | copy-start | bytes 98308
  1.7 1.0 copy-start.2
  2.7 137.9 %copy-start.9 = (s32[1,2048]{1,0:T(1,128)S(1)}, s32[1,2048]{1,0:T(1,128)}, u32[]{:S(2)}) copy-start(s32[1,2048]{1,0:T(1,128)} %param.25) | copy-start | bytes 24580
  4.6 136.0 %copy-start.1 = (f32[2048,128]{1,0:T(8,128)S(1)}, f32[2048,128]{1,0:T(8,128)}, u32[]{:S(2)}) copy-start(f32[2048,128]{1,0:T(8,128)} %param.27) | copy-start | bytes 3145732
  4.6 13.1 %collective-permute-start = (bf16[2048,192]{0,1:T(8,128)(2,1)}, bf16[2048,192]{0,1:T(8,128)(2,1)}, u32[]{:S(2)}, u32[]{:S(2)}) collective-permute-start(bf16[2048,192]{0,1:T(8,128)(2,1)} %pad_maximum_fusion), channel_id=1, source_target_pairs={{0,1},{1,2},{2,3},{3,4},{4,5},{5,6},{6,7},{8,9},{9,10},{10,11},{11... | collective-permute-start | bytes 2359304 | tf_op jit(solution)/shard_map/ppermute | solution.py:12
  8.5 57.3 %collective-permute-start.3 = (bf16[2048,192]{0,1:T(8,128)(2,1)}, bf16[2048,192]{0,1:T(8,128)(2,1)}, u32[]{:S(2)}, u32[]{:S(2)}) collective-permute-start(bf16[2048,192]{0,1:T(8,128)(2,1)} %pad_maximum_fusion), channel_id=1, source_target_pairs={{1,0},{2,1},{3,2},{4,3},{5,4},{6,5},{7,6},{9,8},{10,9},{11,10},{12... | collective-permute-start | bytes 2359304 | tf_op jit(solution)/shard_map/ppermute | solution.py:12
  17.7 50.1 %collective-permute-start.1 = (bf16[2048,192]{0,1:T(8,128)(2,1)}, bf16[2048,192]{0,1:T(8,128)(2,1)}, u32[]{:S(2)}, u32[]{:S(2)}) collective-permute-start(bf16[2048,192]{0,1:T(8,128)(2,1)} %collective-permute-done), channel_id=1, source_target_pairs={{0,1},{1,2},{2,3},{3,4},{4,5},{5,6},{6,7},{8,9},{9,10},{10,11},{11... | collective-permute-start | bytes 2359304 | tf_op jit(solution)/shard_map/ppermute | solution.py:12
  65.8 94.9 %collective-permute-start.4 = (bf16[2048,192]{0,1:T(8,128)(2,1)}, bf16[2048,192]{0,1:T(8,128)(2,1)}, u32[]{:S(2)}, u32[]{:S(2)}) collective-permute-start(bf16[2048,192]{0,1:T(8,128)(2,1)} %collective-permute-done.3), channel_id=1, source_target_pairs={{1,0},{2,1},{3,2},{4,3},{5,4},{6,5},{7,6},{9,8},{10,9},{11,10},{12... | collective-permute-start | bytes 2359304 | tf_op jit(solution)/shard_map/ppermute | solution.py:12
  67.8 102.2 %collective-permute-start.2 = (bf16[2048,192]{0,1:T(8,128)(2,1)}, bf16[2048,192]{0,1:T(8,128)(2,1)}, u32[]{:S(2)}, u32[]{:S(2)}) collective-permute-start(bf16[2048,192]{0,1:T(8,128)(2,1)} %collective-permute-done.1), channel_id=1, source_target_pairs={{0,1},{1,2},{2,3},{3,4},{4,5},{5,6},{6,7},{8,9},{9,10},{10,11},{11... | collective-permute-start | bytes 2359304 | tf_op jit(solution)/shard_map/ppermute | solution.py:12
  140.6 10.2 %copy-start.11 = (s32[1,4]{1,0:T(1,128)S(1)}, s32[1,4]{1,0:T(1,128)}, u32[]{:S(2)}) copy-start(s32[1,4]{1,0:T(1,128)} %param.35) | copy-start | bytes 52
  160.7 21.2 %collective-permute-start.5 = (bf16[2048,192]{0,1:T(8,128)(2,1)}, bf16[2048,192]{0,1:T(8,128)(2,1)S(1)}, u32[]{:S(2)}, u32[]{:S(2)}) collective-permute-start(bf16[2048,192]{0,1:T(8,128)(2,1)} %collective-permute-done.4), channel_id=1, source_target_pairs={{1,0},{2,1},{3,2},{4,3},{5,4},{6,5},{7,6},{9,8},{10,9},{11,10},{12... | collective-permute-start | bytes 2359304 | tf_op jit(solution)/shard_map/ppermute | solution.py:12
  182.8 10.3 %copy-start.12 = (s32[1,8]{1,0:T(1,128)S(1)}, s32[1,8]{1,0:T(1,128)}, u32[]{:S(2)}) copy-start(s32[1,8]{1,0:T(1,128)} %param.33) | copy-start | bytes 100
  193.1 79.7 %copy-start.3 = (f32[2048,128]{0,1:T(8,128)S(1)}, f32[2048,128]{0,1:T(8,128)}, u32[]{:S(2)}) copy-start(f32[2048,128]{0,1:T(8,128)} %copy-done.2) | copy-start | bytes 3145732
  193.1 79.7 %copy-start.6 = (bf16[1,256,256]{2,1,0:T(8,128)(2,1)S(1)}, bf16[1,256,256]{2,1,0:T(8,128)(2,1)}, u32[]{:S(2)}) copy-start(bf16[1,256,256]{2,1,0:T(8,128)(2,1)} %param.30) | copy-start | bytes 393220
  193.1 79.7 %copy-start.7 = (f32[256,128]{0,1:T(8,128)S(1)}, f32[256,128]{0,1:T(8,128)}, u32[]{:S(2)}) copy-start(f32[256,128]{0,1:T(8,128)} %copy.41) | copy-start | bytes 393220
  193.2 79.7 %copy-start.10 = (f32[128]{0:T(128)S(1)}, f32[128]{0:T(128)}, u32[]{:S(2)}) copy-start(f32[128]{0:T(128)} %param.28) | copy-start | bytes 1540
where the time goes:
time: 281 us; the launch traced here: 279 us
  blocking collectives  84 us (30%)
  local copies, waits for them, and re-layouts  66.5 us (24%)
  matrix products  65 us (23%)
  starting transfers between devices  25.7 us (9%)
  other arithmetic  17.5 us (6%)
  loops' own time  12.3 us (4%)
  waiting for transfers between devices  7.31 us (3%)
    dot_general x7, matrix products, include(): jnp.dot(kernel_tile(points, other_points), other_values, preferred_elemen...  56.4 us
    ppermute x6, starting transfers between devices, passed_along(): return lax.ppermute(block, axis, route)  25.7 us
    psum x1, blocking collectives, body(): upper = lax.psum(upward_terms, 'leaf').astype(jnp.bfloat16)  25.1 us
    all_gather x1, blocking collectives, body(): skeletons = lax.all_gather(leaf_skeleton, 'leaf', axis=0, tiled=True)  20 us
    all_gather x1, blocking collectives, body(): values = lax.all_gather(coeffs[None], 'leaf', axis=0, tiled=True)  17.8 us
    reduce_sum x10, other arithmetic, kernel_tile(): right_sq = jnp.sum(right_f * right_f, axis=1)  14.6 us
    all_gather x1, blocking collectives, body(): values = lax.all_gather(upper[None], 'group', axis=0, tiled=True)  13.8 us
    unnamed x32, local copies, waits for them, and re-layouts  13.4 us
  transfers between devices with their start and end apart: 6, of which 1 were waited for; matrix products, arithmetic and copies ran while one was open for 19% of the time, Pallas kernels for 0%

commit v1 on v0

--- a/solution.py
+++ b/solution.py
@@ -101,7 +101,27 @@
         return visit
 
     empty_far = jnp.zeros((rank_cols, rhs_cols), jnp.float32)
-    skeletons = lax.all_gather(leaf_skeleton, "leaf", axis=0, tiled=True)
+    size, here, extent = (lax.axis_size("leaf"), lax.axis_index("leaf"), leaf_skeleton.shape[0])
+    ahead = [(i_2, (i_2 + 1) % size) for i_2 in range(size)]
+    left_2 = [(i_2, (i_2 - 1) % size) for i_2 in range(size)]
+    result = jnp.zeros(
+        (*leaf_skeleton.shape[:0], size * extent, *leaf_skeleton.shape[0 + 1 :]),
+        leaf_skeleton.dtype,
+    )
+    result = lax.dynamic_update_slice_in_dim(result, leaf_skeleton, here * extent, axis=0)
+    from_left = from_right = leaf_skeleton
+    half = size // 2
+    for turn in range(1, half + 1):
+        from_left = lax.ppermute(from_left, "leaf", ahead)
+        result = lax.dynamic_update_slice_in_dim(
+            result, from_left, (here - turn) % size * extent, axis=0
+        )
+        if turn < size - half:
+            from_right = lax.ppermute(from_right, "leaf", left_2)
+            result = lax.dynamic_update_slice_in_dim(
+                result, from_right, (here + turn) % size * extent, axis=0
+            )
+    skeletons = result
     values = lax.all_gather(coeffs[None], "leaf", axis=0, tiled=True)
     far_sum = lax.fori_loop(0, skeletons.shape[0], far_visit(skeletons, values), empty_far)
     upward_terms = lax.dot_general(

time: 281 us -> 263 us (0.936)
  blocking collectives: 84 us -> 64.1 us
  starting transfers between devices: 25.7 us -> 33.8 us
  local copies, waits for them, and re-layouts: 66.5 us -> 59 us
    all_gather x1 -> x0, blocking collectives: 20 us -> none  [body(): skeletons = lax.all_gather(leaf_skeleton, 'leaf', axis=0, tiled=True)]
    ppermute x0 -> x7, waiting for transfers between devices: none -> 9.41 us  [the longest x4 9.4 us: body(): from_left = lax.ppermute(from_left, 'leaf', ahead)]
    ppermute x0 -> x7, starting transfers between devices: none -> 7.74 us  [the longest x4 7.43 us: body(): from_left = lax.ppermute(from_left, 'leaf', ahead)]
    ppermute x6, waiting for transfers between devices: 7.31 us -> 0.02 us  [passed_along(): return lax.ppermute(block, axis, route)]
    all_gather x1, blocking collectives: 13.8 us -> 7.66 us  [body(): values = lax.all_gather(upper[None], 'group', axis=0, tiled=True)]
    dynamic_slice x8, local copies, waits for them, and re-layouts: 9.86 us -> 4.73 us  [visit(): listed = lax.dynamic_index_in_dim(far_row, position, 0, keepdims=False)]
    all_gather x1, blocking collectives: 17.8 us -> 22.4 us  [body(): values = lax.all_gather(coeffs[None], 'leaf', axis=0, tiled=True)]
    unnamed x32 -> x38, local copies, waits for them, and re-layouts: 13.4 us -> 13.3 us
  transfers between devices with their start and end apart: 6 -> 13, of which waited for: 1 -> 2; matrix products, arithmetic and copies ran while one was open for 19% -> 19% of each run, Pallas kernels for 0% -> 0%
where the time goes in v1:
time: 263 us; the launch traced here: 261 us
  blocking collectives  64.1 us (24%)
  matrix products  64 us (24%)
  local copies, waits for them, and re-layouts  59 us (22%)
  starting transfers between devices  33.8 us (13%)
  other arithmetic  17.9 us (7%)
  loops' own time  12.3 us (5%)
  waiting for transfers between devices  9.42 us (4%)
    dot_general x7, matrix products, include(): jnp.dot(kernel_tile(points, other_points), other_values, preferred_elemen...  56.5 us
    psum x1, blocking collectives, body(): upper = lax.psum(upward_terms, 'leaf').astype(jnp.bfloat16)  26.7 us
    ppermute x6, starting transfers between devices, passed_along(): return lax.ppermute(block, axis, route)  26 us
    all_gather x1, blocking collectives, body(): values = lax.all_gather(coeffs[None], 'leaf', axis=0, tiled=True)  22.4 us
    reduce_sum x10, other arithmetic, kernel_tile(): right_sq = jnp.sum(right_f * right_f, axis=1)  13.7 us
    unnamed x38, local copies, waits for them, and re-layouts  13.3 us
    while x3, local copies, waits for them, and re-layouts, body(): lax.fori_loop(0, 2 * reach + 1, window_visit, jnp.zeros((leaf_rows, rhs_c...  11.1 us
    gather x2, local copies, waits for them, and re-layouts, body(): sorted_target = target[ordering[0]]  10.2 us
  transfers between devices with their start and end apart: 13, of which 2 were waited for; matrix products, arithmetic and copies ran while one was open for 19% of the time, Pallas kernels for 0%

profile of v1, /device:TPU:15, one launch (start us, length us, event | category | flops | bytes accessed | tf_op | source)
XLA Modules:
  0.0 260.9 jit_solution(5190310139153603517)
XLA Ops:
  15.0 26.7 %all-reduce.1 = bf16[256,128]{0,1:T(8,128)(2,1)S(1)} all-reduce(f32[256,128]{0,1:T(8,128)S(1)} %convolution_bitcast_fusion.2), channel_id=1, replica_groups=mesh['group'=4,'leaf'=8] {'leaf'}, use_global_device_ids=true, to_apply=%region_6.7 | all-reduce | flops 32768 | bytes 196608 | tf_op jit(solution)/shard_map/psum | solution.py:130
  41.7 7.7 %all-gather.1 = bf16[1024,128]{0,1:T(8,128)(2,1)} all-gather(bf16[256,128]{0,1:T(8,128)(2,1)S(1)} %all-reduce.1), channel_id=3, replica_groups=mesh['group'=4,'leaf'=8] {'group'}, dimensions={0}, use_global_device_ids=true | all-gather | bytes 327680 | tf_op jit(solution)/shard_map/all_gather | solution.py:133
  55.0 22.4 %all-gather = bf16[2048,128]{1,0:T(8,128)(2,1)} all-gather(bf16[256,128]{1,0:T(8,128)(2,1)S(1)} %convolution_convert_fusion), channel_id=2, replica_groups=mesh['group'=4,'leaf'=8] {'leaf'}, dimensions={0}, use_global_device_ids=true | all-gather | bytes 589824 | tf_op jit(solution)/shard_map/all_gather | solution.py:125
  80.4 7.4 %all_gather.10 = bf16[4,256,64]{1,2,0:T(8,128)(2,1)} all-gather(bf16[1,256,64]{1,2,0:T(8,128)(2,1)} %param.32), channel_id=1, replica_groups=mesh['group'=4,'leaf'=8] {'group'}, dimensions={0}, use_global_device_ids=true | all-gather | bytes 163840 | tf_op jit(solution)/shard_map/all_gather | solution.py:132
  89.5 7.6 %gather_fusion = f32[2048,128]{1,0:T(8,128)} fusion(f32[2048,128]{1,0:T(8,128)S(1)} %copy-done.1, s32[2048]{0:T(1024)S(1)} %broadcast_clamp_fusion), kind=kCustom, calls=%fused_computation | custom fusion | bytes 2105344 | tf_op jit(solution)/shard_map/gather | solution.py:152
  99.8 9.7 %while.51 = (s32[]{:T(128)}, f32[256,128]{1,0:T(8,128)S(1)}, s32[4]{0:T(128)S(1)}, bf16[1,256,64]{2,1,0:T(8,128)(2,1)S(1)}, bf16[4,256,64]{2,1,0:T(8,128)(2,1)},...) while((s32[]{:T(128)}, f32[256,128]{1,0:T(8,128)S(1)}, s32[4]{0:T(128)S(1)}, ...), condition=%wide.region_12.13_spmd, body=%wide.region_7.0_spmd.sunk | while | flops 25624072 | bytes 496837 | solution.py:147
  132.1 11.1 %while.50 = (s32[]{:T(128)}, f32[256,128]{1,0:T(8,128)S(1)}, s32[8]{0:T(128)S(1)}, bf16[1,256,64]{2,1,0:T(8,128)(2,1)S(1)}, bf16[8,256,64]{2,1,0:T(8,128)(2,1)S(...) while((s32[]{:T(128)}, f32[256,128]{1,0:T(8,128)S(1)}, s32[8]{0:T(128)S(1)}, ...), condition=%wide.region_5.6_spmd, body=%wide.region_0.5_spmd.sunk | while | flops 25624072 | bytes 529605 | solution.py:126
  144.0 9.4 %collective-permute-start.12 = (bf16[2048,192]{0,1:T(8,128)(2,1)}, bf16[2048,192]{0,1:T(8,128)(2,1)S(1)}, u32[]{:S(2)}, u32[]{:S(2)}) collective-permute-start(bf16[2048,192]{0,1:T(8,128)(2,1)} %collective-permute-done.11), channel_id=1, source_target_pairs={{1,0},{2,1},{3,2},{4,3},{5,4},{6,5},{7,6},{9,8},{10,9},{11,10},{12... | collective-permute-start | bytes 2359304 | tf_op jit(solution)/shard_map/ppermute | solution.py:12
  166.1 9.3 %copy.49 = bf16[14336,192]{1,0:T(8,128)(2,1)} copy(bf16[14336,192]{0,1:T(8,128)(2,1)} %constant_dynamic-update-slice_fusion) | data formatting | bytes 11010048 | tf_op jit(solution)/shard_map/while | solution.py:83
  176.5 77.4 %while.52 = (s32[]{:T(128)}, f32[2048,128]{1,0:T(8,128)}, s32[]{:T(128)}, s32[8]{0:T(128)S(1)}, bf16[2048,64]{1,0:T(8,128)(2,1)S(1)}, /*index=5*/bf16[14336,192]...) while((s32[]{:T(128)}, f32[2048,128]{1,0:T(8,128)}, ...), condition=%wide.region_18.19_spmd, body=%wide.region_13.18_spmd.sunk | while | flops 1632628736 | bytes 3966781 | solution.py:83
  177.9 9.8 %conditional.8 = (f32[2048,128]{1,0:T(8,128)}) conditional(s32[]{:T(128)} %convert_element_type.115, f32[2048,128]{1,0:T(8,128)} %get-tuple-element.708, (bf16[2048,64]{1,0:T(8,128)(2,1)S(1)}, s32[]{:T(128)}, bf16[14336,192]{1,0:T(8,128)(2,1)}, f32[2048,128]{1,0:T(8,128)}) %tuple.139), branch_computations={%region_14.14_spmd, %region_15.17_spmd} | conditional | flops 1632628736 | bytes 3966534 | solution.py:81
  179.5 8.1 %convolution_add_fusion = f32[2048,128]{1,0:T(8,128)} fusion(f32[2048,128]{1,0:T(8,128)} %get-tuple-element.471, bf16[2048,64]{1,0:T(8,128)(2,1)S(1)} %get-tuple-element.472, f32[2048]{0:T(1024)S(1)} %get-tuple-element.582, f32[2048]{0:T(1024)S(1)} %get-tuple-element.583, bf16[14336,192]{1,0:T(8,128)(2,1)} %get-tuple-element.473, s32[]{:T(128)S(6)} %select_n.85, ...), kind=kOutput, calls=%fused_computation.47 | convolution fusion | flops 1631846400 | bytes 3425792 | tf_op jit(solution)/shard_map/while/body/eval_jaxpr/cond/branch_1_fun/dot_general | solution.py:77
  188.9 9.8 %conditional.8 = (f32[2048,128]{1,0:T(8,128)}) conditional(s32[]{:T(128)} %convert_element_type.115, f32[2048,128]{1,0:T(8,128)} %get-tuple-element.708, (bf16[2048,64]{1,0:T(8,128)(2,1)S(1)}, s32[]{:T(128)}, bf16[14336,192]{1,0:T(8,128)(2,1)}, f32[2048,128]{1,0:T(8,128)}) %tuple.139), branch_computations={%region_14.14_spmd, %region_15.17_spmd} | conditional | flops 1632628736 | bytes 3966534 | solution.py:81
  190.6 8.1 %convolution_add_fusion = f32[2048,128]{1,0:T(8,128)} fusion(f32[2048,128]{1,0:T(8,128)} %get-tuple-element.471, bf16[2048,64]{1,0:T(8,128)(2,1)S(1)} %get-tuple-element.472, f32[2048]{0:T(1024)S(1)} %get-tuple-element.582, f32[2048]{0:T(1024)S(1)} %get-tuple-element.583, bf16[14336,192]{1,0:T(8,128)(2,1)} %get-tuple-element.473, s32[]{:T(128)S(6)} %select_n.85, ...), kind=kOutput, calls=%fused_computation.47 | convolution fusion | flops 1631846400 | bytes 3425792 | tf_op jit(solution)/shard_map/while/body/eval_jaxpr/cond/branch_1_fun/dot_general | solution.py:77
  199.9 9.8 %conditional.8 = (f32[2048,128]{1,0:T(8,128)}) conditional(s32[]{:T(128)} %convert_element_type.115, f32[2048,128]{1,0:T(8,128)} %get-tuple-element.708, (bf16[2048,64]{1,0:T(8,128)(2,1)S(1)}, s32[]{:T(128)}, bf16[14336,192]{1,0:T(8,128)(2,1)}, f32[2048,128]{1,0:T(8,128)}) %tuple.139), branch_computations={%region_14.14_spmd, %region_15.17_spmd} | conditional | flops 1632628736 | bytes 3966534 | solution.py:81
  201.6 8.1 %convolution_add_fusion = f32[2048,128]{1,0:T(8,128)} fusion(f32[2048,128]{1,0:T(8,128)} %get-tuple-element.471, bf16[2048,64]{1,0:T(8,128)(2,1)S(1)} %get-tuple-element.472, f32[2048]{0:T(1024)S(1)} %get-tuple-element.582, f32[2048]{0:T(1024)S(1)} %get-tuple-element.583, bf16[14336,192]{1,0:T(8,128)(2,1)} %get-tuple-element.473, s32[]{:T(128)S(6)} %select_n.85, ...), kind=kOutput, calls=%fused_computation.47 | convolution fusion | flops 1631846400 | bytes 3425792 | tf_op jit(solution)/shard_map/while/body/eval_jaxpr/cond/branch_1_fun/dot_general | solution.py:77
  211.0 9.8 %conditional.8 = (f32[2048,128]{1,0:T(8,128)}) conditional(s32[]{:T(128)} %convert_element_type.115, f32[2048,128]{1,0:T(8,128)} %get-tuple-element.708, (bf16[2048,64]{1,0:T(8,128)(2,1)S(1)}, s32[]{:T(128)}, bf16[14336,192]{1,0:T(8,128)(2,1)}, f32[2048,128]{1,0:T(8,128)}) %tuple.139), branch_computations={%region_14.14_spmd, %region_15.17_spmd} | conditional | flops 1632628736 | bytes 3966534 | solution.py:81
  212.7 8.1 %convolution_add_fusion = f32[2048,128]{1,0:T(8,128)} fusion(f32[2048,128]{1,0:T(8,128)} %get-tuple-element.471, bf16[2048,64]{1,0:T(8,128)(2,1)S(1)} %get-tuple-element.472, f32[2048]{0:T(1024)S(1)} %get-tuple-element.582, f32[2048]{0:T(1024)S(1)} %get-tuple-element.583, bf16[14336,192]{1,0:T(8,128)(2,1)} %get-tuple-element.473, s32[]{:T(128)S(6)} %select_n.85, ...), kind=kOutput, calls=%fused_computation.47 | convolution fusion | flops 1631846400 | bytes 3425792 | tf_op jit(solution)/shard_map/while/body/eval_jaxpr/cond/branch_1_fun/dot_general | solution.py:77
  222.0 9.8 %conditional.8 = (f32[2048,128]{1,0:T(8,128)}) conditional(s32[]{:T(128)} %convert_element_type.115, f32[2048,128]{1,0:T(8,128)} %get-tuple-element.708, (bf16[2048,64]{1,0:T(8,128)(2,1)S(1)}, s32[]{:T(128)}, bf16[14336,192]{1,0:T(8,128)(2,1)}, f32[2048,128]{1,0:T(8,128)}) %tuple.139), branch_computations={%region_14.14_spmd, %region_15.17_spmd} | conditional | flops 1632628736 | bytes 3966534 | solution.py:81
  223.7 8.1 %convolution_add_fusion = f32[2048,128]{1,0:T(8,128)} fusion(f32[2048,128]{1,0:T(8,128)} %get-tuple-element.471, bf16[2048,64]{1,0:T(8,128)(2,1)S(1)} %get-tuple-element.472, f32[2048]{0:T(1024)S(1)} %get-tuple-element.582, f32[2048]{0:T(1024)S(1)} %get-tuple-element.583, bf16[14336,192]{1,0:T(8,128)(2,1)} %get-tuple-element.473, s32[]{:T(128)S(6)} %select_n.85, ...), kind=kOutput, calls=%fused_computation.47 | convolution fusion | flops 1631846400 | bytes 3425792 | tf_op jit(solution)/shard_map/while/body/eval_jaxpr/cond/branch_1_fun/dot_general | solution.py:77
  233.1 9.8 %conditional.8 = (f32[2048,128]{1,0:T(8,128)}) conditional(s32[]{:T(128)} %convert_element_type.115, f32[2048,128]{1,0:T(8,128)} %get-tuple-element.708, (bf16[2048,64]{1,0:T(8,128)(2,1)S(1)}, s32[]{:T(128)}, bf16[14336,192]{1,0:T(8,128)(2,1)}, f32[2048,128]{1,0:T(8,128)}) %tuple.139), branch_computations={%region_14.14_spmd, %region_15.17_spmd} | conditional | flops 1632628736 | bytes 3966534 | solution.py:81
  234.7 8.1 %convolution_add_fusion = f32[2048,128]{1,0:T(8,128)} fusion(f32[2048,128]{1,0:T(8,128)} %get-tuple-element.471, bf16[2048,64]{1,0:T(8,128)(2,1)S(1)} %get-tuple-element.472, f32[2048]{0:T(1024)S(1)} %get-tuple-element.582, f32[2048]{0:T(1024)S(1)} %get-tuple-element.583, bf16[14336,192]{1,0:T(8,128)(2,1)} %get-tuple-element.473, s32[]{:T(128)S(6)} %select_n.85, ...), kind=kOutput, calls=%fused_computation.47 | convolution fusion | flops 1631846400 | bytes 3425792 | tf_op jit(solution)/shard_map/while/body/eval_jaxpr/cond/branch_1_fun/dot_general | solution.py:77
  244.1 9.8 %conditional.8 = (f32[2048,128]{1,0:T(8,128)}) conditional(s32[]{:T(128)} %convert_element_type.115, f32[2048,128]{1,0:T(8,128)} %get-tuple-element.708, (bf16[2048,64]{1,0:T(8,128)(2,1)S(1)}, s32[]{:T(128)}, bf16[14336,192]{1,0:T(8,128)(2,1)}, f32[2048,128]{1,0:T(8,128)}) %tuple.139), branch_computations={%region_14.14_spmd, %region_15.17_spmd} | conditional | flops 1632628736 | bytes 3966534 | solution.py:81
  245.8 8.1 %convolution_add_fusion = f32[2048,128]{1,0:T(8,128)} fusion(f32[2048,128]{1,0:T(8,128)} %get-tuple-element.471, bf16[2048,64]{1,0:T(8,128)(2,1)S(1)} %get-tuple-element.472, f32[2048]{0:T(1024)S(1)} %get-tuple-element.582, f32[2048]{0:T(1024)S(1)} %get-tuple-element.583, bf16[14336,192]{1,0:T(8,128)(2,1)} %get-tuple-element.473, s32[]{:T(128)S(6)} %select_n.85, ...), kind=kOutput, calls=%fused_computation.47 | convolution fusion | flops 1631846400 | bytes 3425792 | tf_op jit(solution)/shard_map/while/body/eval_jaxpr/cond/branch_1_fun/dot_general | solution.py:77
  (137 shorter events, 107.5 us)
Async XLA Ops:
  0.0 77.4 %copy-start.3 = (bf16[2048,64]{0,1:T(8,128)(2,1)S(1)}, bf16[2048,64]{0,1:T(8,128)(2,1)}, u32[]{:S(2)}) copy-start(bf16[2048,64]{0,1:T(8,128)(2,1)} %param.24) | copy-start | bytes 786436
  0.0 55.0 %copy-start.11 = (s32[1,2048]{1,0:T(1,128)S(1)}, s32[1,2048]{1,0:T(1,128)}, u32[]{:S(2)}) copy-start(s32[1,2048]{1,0:T(1,128)} %param.25) | copy-start | bytes 24580
  1.0 88.5 %copy-start.1 = (f32[2048,128]{1,0:T(8,128)S(1)}, f32[2048,128]{1,0:T(8,128)}, u32[]{:S(2)}) copy-start(f32[2048,128]{1,0:T(8,128)} %param.27) | copy-start | bytes 3145732
  1.0 108.4 %collective-permute-start = (bf16[1,256,64]{2,1,0:T(8,128)(2,1)S(1)}, bf16[1,256,64]{2,1,0:T(8,128)(2,1)}, u32[]{:S(2)}, u32[]{:S(2)}) collective-permute-start(bf16[1,256,64]{2,1,0:T(8,128)(2,1)S(1)} %copy.43), channel_id=1, source_target_pairs={{0,1},{1,2},{2,3},{3,4},{4,5},{5,6},{6,7},{7,0},{8,9},{9,10},{10,1... | collective-permute-start | bytes 98312 | tf_op jit(solution)/shard_map/ppermute | solution.py:115
  2.9 108.4 %collective-permute-start.1 = (bf16[1,256,64]{2,1,0:T(8,128)(2,1)S(1)}, bf16[1,256,64]{2,1,0:T(8,128)(2,1)}, u32[]{:S(2)}, u32[]{:S(2)}) collective-permute-start(bf16[1,256,64]{2,1,0:T(8,128)(2,1)S(1)} %copy.43), channel_id=1, source_target_pairs={{0,7},{1,0},{2,1},{3,2},{4,3},{5,4},{6,5},{7,6},{8,15},{9,8},{10,9... | collective-permute-start | bytes 98312 | tf_op jit(solution)/shard_map/ppermute | solution.py:120
  8.6 40.8 %collective-permute-start.7 = (bf16[2048,192]{0,1:T(8,128)(2,1)}, bf16[2048,192]{0,1:T(8,128)(2,1)}, u32[]{:S(2)}, u32[]{:S(2)}) collective-permute-start(bf16[2048,192]{0,1:T(8,128)(2,1)} %pad_maximum_fusion), channel_id=1, source_target_pairs={{0,1},{1,2},{2,3},{3,4},{4,5},{5,6},{6,7},{8,9},{9,10},{10,11},{11... | collective-permute-start | bytes 2359304 | tf_op jit(solution)/shard_map/ppermute | solution.py:12
  12.3 99.4 %collective-permute-start.10 = (bf16[2048,192]{0,1:T(8,128)(2,1)}, bf16[2048,192]{0,1:T(8,128)(2,1)}, u32[]{:S(2)}, u32[]{:S(2)}) collective-permute-start(bf16[2048,192]{0,1:T(8,128)(2,1)} %pad_maximum_fusion), channel_id=1, source_target_pairs={{1,0},{2,1},{3,2},{4,3},{5,4},{6,5},{7,6},{9,8},{10,9},{11,10},{12... | collective-permute-start | bytes 2359304 | tf_op jit(solution)/shard_map/ppermute | solution.py:12
  49.4 28.0 %copy-start.4 = (bf16[8,256,64]{2,1,0:T(8,128)(2,1)}, bf16[8,256,64]{2,1,0:T(8,128)(2,1)S(1)}, u32[]{:S(2)}) copy-start(bf16[8,256,64]{2,1,0:T(8,128)(2,1)S(1)} %constant_dynamic-update-slice_fusion.14) | copy-start | bytes 786436
  49.4 65.8 %collective-permute-start.8 = (bf16[2048,192]{0,1:T(8,128)(2,1)}, bf16[2048,192]{0,1:T(8,128)(2,1)}, u32[]{:S(2)}, u32[]{:S(2)}) collective-permute-start(bf16[2048,192]{0,1:T(8,128)(2,1)} %collective-permute-done.7), channel_id=1, source_target_pairs={{0,1},{1,2},{2,3},{3,4},{4,5},{5,6},{6,7},{8,9},{9,10},{10,11},{11... | collective-permute-start | bytes 2359304 | tf_op jit(solution)/shard_map/ppermute | solution.py:12
  97.1 35.0 %copy-start.14 = (s32[1,8]{1,0:T(1,128)S(1)}, s32[1,8]{1,0:T(1,128)}, u32[]{:S(2)}) copy-start(s32[1,8]{1,0:T(1,128)} %param.34) | copy-start | bytes 100
  109.4 34.6 %copy-start.9 = (f32[256,128]{1,0:T(8,128)}, f32[256,128]{1,0:T(8,128)S(1)}, u32[]{:S(2)}) copy-start(f32[256,128]{1,0:T(8,128)S(1)} %get-tuple-element.486) | copy-start | bytes 393220
  109.4 9.5 %collective-permute-start.2 = (bf16[1,256,64]{2,1,0:T(8,128)(2,1)}, bf16[1,256,64]{2,1,0:T(8,128)(2,1)S(1)}, u32[]{:S(2)}, u32[]{:S(2)}) collective-permute-start(bf16[1,256,64]{2,1,0:T(8,128)(2,1)} %collective-permute-done), channel_id=1, source_target_pairs={{0,1},{1,2},{2,3},{3,4},{4,5},{5,6},{6,7},{7,0},{8,9},{9,10},{10,1... | collective-permute-start | bytes 98312 | tf_op jit(solution)/shard_map/ppermute | solution.py:115
  111.3 8.6 %collective-permute-start.3 = (bf16[1,256,64]{2,1,0:T(8,128)(2,1)}, bf16[1,256,64]{2,1,0:T(8,128)(2,1)S(1)}, u32[]{:S(2)}, u32[]{:S(2)}) collective-permute-start(bf16[1,256,64]{2,1,0:T(8,128)(2,1)} %collective-permute-done.1), channel_id=1, source_target_pairs={{0,7},{1,0},{2,1},{3,2},{4,3},{5,4},{6,5},{7,6},{8,15},{9,8},{10,9... | collective-permute-start | bytes 98312 | tf_op jit(solution)/shard_map/ppermute | solution.py:120
  111.7 32.3 %collective-permute-start.11 = (bf16[2048,192]{0,1:T(8,128)(2,1)}, bf16[2048,192]{0,1:T(8,128)(2,1)}, u32[]{:S(2)}, u32[]{:S(2)}) collective-permute-start(bf16[2048,192]{0,1:T(8,128)(2,1)} %collective-permute-done.10), channel_id=1, source_target_pairs={{1,0},{2,1},{3,2},{4,3},{5,4},{6,5},{7,6},{9,8},{10,9},{11,10},{12... | collective-permute-start | bytes 2359304 | tf_op jit(solution)/shard_map/ppermute | solution.py:12
  115.2 38.2 %collective-permute-start.9 = (bf16[2048,192]{0,1:T(8,128)(2,1)}, bf16[2048,192]{0,1:T(8,128)(2,1)}, u32[]{:S(2)}, u32[]{:S(2)}) collective-permute-start(bf16[2048,192]{0,1:T(8,128)(2,1)} %collective-permute-done.8), channel_id=1, source_target_pairs={{0,1},{1,2},{2,3},{3,4},{4,5},{5,6},{6,7},{8,9},{9,10},{10,11},{11... | collective-permute-start | bytes 2359304 | tf_op jit(solution)/shard_map/ppermute | solution.py:12
  119.0 8.2 %collective-permute-start.4 = (bf16[1,256,64]{2,1,0:T(8,128)(2,1)S(1)}, bf16[1,256,64]{2,1,0:T(8,128)(2,1)S(1)}, u32[]{:S(2)}, u32[]{:S(2)}) collective-permute-start(bf16[1,256,64]{2,1,0:T(8,128)(2,1)S(1)} %collective-permute-done.2), channel_id=1, source_target_pairs={{0,1},{1,2},{2,3},{3,4},{4,5},{5,6},{6,7},{7,0},{8,9},{9,10},{10,1... | collective-permute-start | bytes 98312 | tf_op jit(solution)/shard_map/ppermute | solution.py:115
  120.0 9.9 %collective-permute-start.5 = (bf16[1,256,64]{2,1,0:T(8,128)(2,1)S(1)}, bf16[1,256,64]{2,1,0:T(8,128)(2,1)S(1)}, u32[]{:S(2)}, u32[]{:S(2)}) collective-permute-start(bf16[1,256,64]{2,1,0:T(8,128)(2,1)S(1)} %collective-permute-done.3), channel_id=1, source_target_pairs={{0,7},{1,0},{2,1},{3,2},{4,3},{5,4},{6,5},{7,6},{8,15},{9,8},{10,9... | collective-permute-start | bytes 98312 | tf_op jit(solution)/shard_map/ppermute | solution.py:120
  127.2 4.9 %collective-permute-start.6 = (bf16[1,256,64]{2,1,0:T(8,128)(2,1)S(1)}, bf16[1,256,64]{2,1,0:T(8,128)(2,1)S(1)}, u32[]{:S(2)}, u32[]{:S(2)}) collective-permute-start(bf16[1,256,64]{2,1,0:T(8,128)(2,1)S(1)} %collective-permute-done.4), channel_id=1, source_target_pairs={{0,1},{1,2},{2,3},{3,4},{4,5},{5,6},{6,7},{7,0},{8,9},{9,10},{10,1... | collective-permute-start | bytes 98312 | tf_op jit(solution)/shard_map/ppermute | solution.py:115
  144.0 21.1 %collective-permute-start.12 = (bf16[2048,192]{0,1:T(8,128)(2,1)}, bf16[2048,192]{0,1:T(8,128)(2,1)S(1)}, u32[]{:S(2)}, u32[]{:S(2)}) collective-permute-start(bf16[2048,192]{0,1:T(8,128)(2,1)} %collective-permute-done.11), channel_id=1, source_target_pairs={{1,0},{2,1},{3,2},{4,3},{5,4},{6,5},{7,6},{9,8},{10,9},{11,10},{12... | collective-permute-start | bytes 2359304 | tf_op jit(solution)/shard_map/ppermute | solution.py:12
  176.5 78.9 %copy-start.2 = (f32[2048,128]{0,1:T(8,128)S(1)}, f32[2048,128]{0,1:T(8,128)}, u32[]{:S(2)}) copy-start(f32[2048,128]{0,1:T(8,128)} %copy.52) | copy-start | bytes 3145732
  176.5 79.0 %copy-start.7 = (bf16[1,256,256]{2,1,0:T(8,128)(2,1)S(1)}, bf16[1,256,256]{2,1,0:T(8,128)(2,1)}, u32[]{:S(2)}) copy-start(bf16[1,256,256]{2,1,0:T(8,128)(2,1)} %param.30) | copy-start | bytes 393220
  176.5 79.0 %copy-start.8 = (f32[256,128]{0,1:T(8,128)S(1)}, f32[256,128]{0,1:T(8,128)}, u32[]{:S(2)}) copy-start(f32[256,128]{0,1:T(8,128)} %copy.47) | copy-start | bytes 393220
  176.5 79.0 %copy-start.10 = (f32[256,128]{1,0:T(8,128)S(1)}, f32[256,128]{1,0:T(8,128)}, u32[]{:S(2)}) copy-start(f32[256,128]{1,0:T(8,128)} %copy-done.9) | copy-start | bytes 393220
  176.5 79.0 %copy-start.12 = (f32[128]{0:T(128)S(1)}, f32[128]{0:T(128)}, u32[]{:S(2)}) copy-start(f32[128]{0:T(128)} %param.28) | copy-start | bytes 1540
  (5 other events, 69.8 us)
